TPU v7x, 32 devices: a whole 2x2x4 slice. The times are simulated.
32 devices in a mesh: ctx: 16 (over z, x, core), head: 2 (over y).
Axes of the slice: x: 2, y: 2, z: 4, core: 2. Of those that a mesh axis runs over, the one named last changes fastest.
Arguments:
- query_heads: bfloat16 [2048, 64, 576], P('ctx', 'head'), may hold values from -16 to 16
- key_latent: bfloat16 [2048, 576], P('ctx'), may hold values from -6 to 6
- doc_start: int32 [2048], P('ctx'), may hold values from 0 to 2047, as said below
- out_grad: bfloat16 [2048, 64, 512], P('ctx', 'head'), may hold values from -12 to 12
Outputs:
- attention: bfloat16 [2048, 64, 512], P('ctx', 'head')
- d_query: bfloat16 [2048, 64, 576], P('ctx', 'head')
- d_key: float32 [2048, 576], P(('ctx', 'head'))
Inputs may be any that keep to these rules, and one draw needn't show every extreme that they name: doc_start[t] <= t; doc_start[t] is t or doc_start[t - 1]; every document holds at most 256 tokens, and some document holds exactly 256.
All inputs are finite; a program needn't handle non-finite values.
Results may differ from a plain program's by a relative error of at most 0.013.
Values may be sent and summed in bfloat16 or wider, within the bound.
A program may use at most 128 MiB of HBM per device.

v0:
```python
from functools import partial

import jax
import jax.numpy as jnp
from jax import lax
from jax.experimental import pallas as pl
from jax.experimental.pallas import tpu as pltpu
from jax.sharding import PartitionSpec as P

MAXDOC = 256
LANES = 128
ALIGN = 16

score_scale = 192 ** (-0.5)
log2_e = 1.4426950408889634


def dot(left, right, dims):
    return lax.dot_general(left, right, (dims, ((), ())), preferred_element_type=jnp.float32)


def window(first_ref, tokens, reach_rows, span, tile):
    origin = lax.axis_index("ctx") * (first_ref.shape[0]) - reach_rows
    low = (first_ref[tile * tokens] - origin) // ALIGN * ALIGN
    need = reach_rows + (tile + 1) * tokens - low
    return origin, low, need


def for_width(first_ref, tokens, reach_rows, span, tile, body):
    origin, low, need = window(first_ref, tokens, reach_rows, span, tile)
    for width in range(LANES, span + 1, LANES):
        fits = need <= width
        if width == LANES:
            chosen = fits
        elif width == span:
            chosen = need > width - LANES
        else:
            chosen = fits & (need > width - LANES)

        @pl.when(chosen)
        def _(width=width):
            start = pl.multiple_of(jnp.minimum(low, span - width), ALIGN)
            body(origin, start, width)


def probs_and_grads(first_ref, q, g, keys, bias_ref, tokens, heads, reach_rows, tile, origin, start, width):
    latent = g.shape[1]
    column = lax.broadcasted_iota(jnp.int32, (1, width), 1) + start
    for t in range(tokens):
        first = first_ref[tile * tokens + t] - origin
        own = reach_rows + tile * tokens + t
        seen = (column >= first) & (column <= own)
        bias_ref[pl.ds(t, 1), :width] = jnp.where(seen, 0.0, -jnp.inf)
    scores = dot(q, keys, ((1,), (1,))) * (score_scale * log2_e)
    scores = scores.reshape(tokens, heads, width) + bias_ref[:, :width][:, None, :]
    scores = scores.reshape(tokens * heads, width)
    top = jnp.max(scores, axis=1, keepdims=True)
    expon = jnp.exp2(scores - top)
    probs = expon * (1.0 / jnp.sum(expon, axis=1, keepdims=True))
    weights = probs.astype(jnp.bfloat16)
    dprob = dot(g, keys[:, :latent], ((1,), (1,)))
    delta = jnp.sum(probs * dprob, axis=1, keepdims=True)
    dscore = (score_scale * probs * (dprob - delta)).astype(jnp.bfloat16)
    return weights, dscore


def whole_kernel(tokens, heads, reach_rows, first_ref, q_ref, g_ref, k_ref, att_ref, dq_ref, dk_ref, bias_ref, acc_ref):
    tile = pl.program_id(0)
    span = k_ref.shape[0]
    latent = g_ref.shape[1]

    @pl.when(tile == 0)
    def _():
        acc_ref[...] = jnp.zeros_like(acc_ref)

    def body(origin, start, width):
        q = q_ref[...]
        g = g_ref[...]
        rows = pl.ds(start, width)
        keys = k_ref[rows, :]
        weights, dscore = probs_and_grads(
            first_ref, q, g, keys, bias_ref, tokens, heads, reach_rows, tile, origin, start, width
        )
        acc_ref[rows, :] += dot(dscore, q, ((0,), (0,)))
        acc_ref[rows, :latent] += dot(weights, g, ((0,), (0,)))
        att_ref[...] = dot(weights, keys[:, :latent], ((1,), (0,))).astype(att_ref.dtype)
        dq_ref[...] = dot(dscore, keys, ((1,), (0,))).astype(dq_ref.dtype)

    for_width(first_ref, tokens, reach_rows, span, tile, body)

    @pl.when(tile == pl.num_programs(0) - 1)
    def _():
        dk_ref[...] = acc_ref[...].astype(dk_ref.dtype)


def attend(q, g, keys, doc_start, heads, tokens):
    rows, width = q.shape
    latent = g.shape[1]
    span = keys.shape[0]
    block_rows = doc_start.shape[0]
    tile_rows = tokens * heads
    row_spec = lambda columns: pl.BlockSpec((tile_rows, columns), lambda i, first: (i, 0))
    full = pl.BlockSpec((span, width), lambda i, first: (0, 0))
    return pl.pallas_call(
        partial(whole_kernel, tokens, heads, span - block_rows),
        grid_spec=pltpu.PrefetchScalarGridSpec(
            num_scalar_prefetch=1,
            grid=(block_rows // tokens,),
            in_specs=[row_spec(width), row_spec(latent), full],
            out_specs=[row_spec(latent), row_spec(width), full],
            scratch_shapes=[
                pltpu.VMEM((tokens, span), jnp.float32),
                pltpu.VMEM((span, width), jnp.float32),
            ],
        ),
        out_shape=[
            jax.ShapeDtypeStruct((rows, latent), jnp.bfloat16),
            jax.ShapeDtypeStruct((rows, width), jnp.bfloat16),
            jax.ShapeDtypeStruct((span, width), jnp.bfloat16),
        ],
        compiler_params=pltpu.CompilerParams(
            dimension_semantics=("arbitrary",), vmem_limit_bytes=60 * 1024 * 1024
        ),
        name="attend",
    )(doc_start, q, g, keys)


def at(ctx_index, head_index):
    return {"ctx": ctx_index, "head": head_index}


def greet(partners):
    barrier = pltpu.get_barrier_semaphore()
    for present, place in partners:

        @pl.when(present)
        def _(place=place):
            pl.semaphore_signal(
                barrier, inc=1, device_id=place, device_id_type=pl.DeviceIdType.MESH
            )

    pl.semaphore_wait(barrier, sum(jnp.where(present, 1, 0) for present, _ in partners))


def unit(size):
    row = lax.broadcasted_iota(jnp.int32, (size, size), 0)
    column = lax.broadcasted_iota(jnp.int32, (size, size), 1)
    return (row == column).astype(jnp.bfloat16)


def gather_kernel(reach, count, k_ref, q_ref, keys_ref, out_ref, held, turned, send_sem, recv_sem):
    step = pl.program_id(0)
    me = lax.axis_index("ctx")
    head = lax.axis_index("head")
    group, width, tokens = q_ref.shape

    def copy(offset):
        return pltpu.make_async_remote_copy(
            src_ref=k_ref,
            dst_ref=held.at[offset - 1],
            send_sem=send_sem.at[offset - 1],
            recv_sem=recv_sem.at[offset - 1],
            device_id=at(jnp.minimum(me + offset, count - 1), head),
            device_id_type=pl.DeviceIdType.MESH,
        )

    offsets = range(1, reach + 1)

    @pl.when(step == 0)
    def _():
        greet(
            [(me + offset < count, at(jnp.minimum(me + offset, count - 1), head)) for offset in offsets]
            + [(me >= offset, at(jnp.maximum(me - offset, 0), head)) for offset in offsets]
        )
        for offset in offsets:

            @pl.when(me + offset < count)
            def _(offset=offset):
                copy(offset).start()

    eye = unit(tokens)
    for h in range(group):
        rows = dot(eye, q_ref[h], ((1,), (1,)))
        for c in range(pl.cdiv(width, LANES)):
            size = min(LANES, width - c * LANES)
            part = rows[:, c * LANES : c * LANES + size]
            if size < LANES:
                part = jnp.concatenate([part, jnp.zeros((tokens, LANES - size), jnp.float32)], axis=1)
            turned[c, pl.ds(h, tokens, stride=group), :] = part
    for c in range(pl.cdiv(width, LANES)):
        size = min(LANES, width - c * LANES)
        part = turned[c].reshape(tokens, group, LANES).astype(jnp.bfloat16)
        out_ref[:, :, c * LANES : c * LANES + size] = part[:, :, :size]

    @pl.when(step == pl.num_programs(0) - 1)
    def _():
        keys_ref[reach * tokens :, :] = dot(eye, k_ref[...], ((1,), (1,))).astype(jnp.bfloat16)
        for offset in offsets:
            place = pl.ds((reach - offset) * tokens, tokens)

            @pl.when(me >= offset)
            def _(offset=offset, place=place):
                copy(offset).wait_recv()
                keys_ref[place, :] = dot(eye, held[offset - 1], ((1,), (1,))).astype(jnp.bfloat16)

            @pl.when(me < offset)
            def _(place=place):
                keys_ref[place, :] = jnp.zeros((tokens, width), jnp.bfloat16)

            @pl.when(me + offset < count)
            def _(offset=offset):
                copy(offset).wait_send()


def gather(keys, queries, reach, group):
    heads, width, tokens = queries.shape
    return pl.pallas_call(
        partial(gather_kernel, reach, lax.axis_size("ctx")),
        grid=(heads // group,),
        in_specs=[
            pl.BlockSpec((width, tokens), lambda i: (0, 0)),
            pl.BlockSpec((group, width, tokens), lambda i: (i, 0, 0)),
        ],
        out_specs=[
            pl.BlockSpec(((reach + 1) * tokens, width), lambda i: (0, 0)),
            pl.BlockSpec((tokens, group, width), lambda i: (0, i, 0)),
        ],
        out_shape=[
            jax.ShapeDtypeStruct(((reach + 1) * tokens, width), jnp.bfloat16),
            jax.ShapeDtypeStruct((tokens, heads, width), jnp.bfloat16),
        ],
        scratch_shapes=[
            pltpu.VMEM((reach, width, tokens), jnp.bfloat16),
            pltpu.VMEM((pl.cdiv(width, LANES), tokens * group, LANES), jnp.float32),
            pltpu.SemaphoreType.DMA((reach,)),
            pltpu.SemaphoreType.DMA((reach,)),
        ],
        compiler_params=pltpu.CompilerParams(
            dimension_semantics=("arbitrary",),
            collective_id=0,
            has_side_effects=True,
            vmem_limit_bytes=60 * 1024 * 1024,
        ),
        name="gather_relay",
    )(keys, queries)


def scatter_kernel(reach, count, head_count, part_ref, dq_ref, out_ref, turned_ref, held, wide, send_sem, recv_sem):
    step = pl.program_id(0)
    me = lax.axis_index("ctx")
    head = lax.axis_index("head")
    own_rows = out_ref.shape[0]
    block_rows = own_rows * head_count
    turns = [(offset, turn) for offset in range(reach, -1, -1) for turn in range(head_count) if offset or turn]

    def rows(offset, owner):
        start = (reach - offset) * block_rows + owner * own_rows
        return pl.ds(pl.multiple_of(start, ALIGN), own_rows)

    def copy(offset, turn):
        target = (head + turn) % head_count
        slot = offset * head_count + turn
        return pltpu.make_async_remote_copy(
            src_ref=part_ref.at[rows(offset, target), :],
            dst_ref=held.at[slot],
            send_sem=send_sem.at[slot],
            recv_sem=recv_sem.at[slot],
            device_id=at(jnp.maximum(me - offset, 0), target),
            device_id_type=pl.DeviceIdType.MESH,
        )

    @pl.when(step == 0)
    def _():
        greet(
            [(me >= offset, at(jnp.maximum(me - offset, 0), (head + turn) % head_count)) for offset, turn in turns]
            + [
                (
                    me + offset < count,
                    at(jnp.minimum(me + offset, count - 1), (head - turn + head_count) % head_count),
                )
                for offset, turn in turns
            ]
        )
        for offset, turn in turns:

            @pl.when(me >= offset)
            def _(offset=offset, turn=turn):
                copy(offset, turn).start()

    tokens, group, width = dq_ref.shape
    for c in range(pl.cdiv(width, LANES)):
        size = min(LANES, width - c * LANES)
        part = dq_ref[:, :, c * LANES : c * LANES + size].astype(jnp.float32)
        if size < LANES:
            part = jnp.concatenate([part, jnp.zeros((tokens, group, LANES - size), jnp.float32)], axis=2)
        wide[c] = part.reshape(tokens * group, LANES)
    for h in range(group):
        for c in range(pl.cdiv(width, LANES)):
            size = min(LANES, width - c * LANES)
            part = wide[c, pl.ds(h, tokens, stride=group), :]
            turned_ref[h, c * LANES : c * LANES + size, :] = part.astype(jnp.bfloat16).T[:size]

    @pl.when(step == pl.num_programs(0) - 1)
    def _():
        for offset, turn in turns:

            @pl.when(me + offset >= count)
            def _(offset=offset, turn=turn):
                held[offset * head_count + turn] = jnp.zeros(held.shape[1:], held.dtype)

        out_ref[...] = part_ref[rows(0, head), :].astype(jnp.float32)
        for offset, turn in turns[::-1]:

            @pl.when(me + offset < count)
            def _(offset=offset, turn=turn):
                copy(offset, turn).wait_recv()

            out_ref[...] += held[offset * head_count + turn].astype(jnp.float32)
        for offset, turn in turns:

            @pl.when(me >= offset)
            def _(offset=offset, turn=turn):
                copy(offset, turn).wait_send()


def scatter(partials, d_query, block_rows, reach, group):
    head_count = lax.axis_size("head")
    tokens, heads, width = d_query.shape
    own_rows = block_rows // head_count
    slots = (reach + 1) * head_count
    return pl.pallas_call(
        partial(scatter_kernel, reach, lax.axis_size("ctx"), head_count),
        grid=(heads // group,),
        in_specs=[
            pl.BlockSpec(partials.shape, lambda i: (0, 0)),
            pl.BlockSpec((tokens, group, width), lambda i: (0, i, 0)),
        ],
        out_specs=[
            pl.BlockSpec((own_rows, width), lambda i: (0, 0)),
            pl.BlockSpec((group, width, tokens), lambda i: (i, 0, 0)),
        ],
        out_shape=[
            jax.ShapeDtypeStruct((own_rows, width), jnp.float32),
            jax.ShapeDtypeStruct((heads, width, tokens), jnp.bfloat16),
        ],
        scratch_shapes=[
            pltpu.VMEM((slots, own_rows, width), jnp.bfloat16),
            pltpu.VMEM((pl.cdiv(width, LANES), tokens * group, LANES), jnp.float32),
            pltpu.SemaphoreType.DMA((slots,)),
            pltpu.SemaphoreType.DMA((slots,)),
        ],
        compiler_params=pltpu.CompilerParams(
            dimension_semantics=("arbitrary",),
            collective_id=1,
            has_side_effects=True,
            vmem_limit_bytes=60 * 1024 * 1024,
        ),
        name="scatter_grads",
    )(partials, d_query)


def shards(query_heads, key_latent, doc_start, out_grad):
    block_rows, head_count, width = query_heads.shape
    latent = out_grad.shape[2]
    reach = (MAXDOC + block_rows - 2) // block_rows
    group = 8
    keys, queries = gather(key_latent.T, query_heads.transpose(1, 2, 0), reach, group)
    rows = block_rows * head_count
    attention, d_query, partials = attend(
        queries.reshape(rows, width),
        out_grad.reshape(rows, latent),
        keys,
        doc_start,
        head_count,
        32,
    )
    d_key, turned = scatter(
        partials, d_query.reshape(block_rows, head_count, width), block_rows, reach, group
    )
    return (attention.reshape(block_rows, head_count, latent), turned.transpose(2, 0, 1), d_key)


def solution(mesh):
    return jax.shard_map(
        shards,
        mesh=mesh,
        in_specs=(P("ctx", "head", None), P("ctx", None), P("ctx"), P("ctx", "head", None)),
        out_specs=(P("ctx", "head", None), P("ctx", "head", None), P(("ctx", "head"), None)),
        check_vma=False,
    )
```

profile of v0, /device:TPU:1, one launch (start us, length us, event | category | flops | bytes accessed | tf_op | source)
XLA Modules:
  0.0 46.0 jit_solution(3919008135453288795)
XLA Ops:
  0.6 10.6 %gather_relay.1 = (bf16[384,576]{1,0:T(8,128)(2,1)}, bf16[128,32,576]{2,1,0:T(8,128)(2,1)}) custom-call(bf16[576,128]{1,0:T(8,128)(2,1)} %bitcast.12, bf16[32,576,128]{2,1,0:T(8,128)(2,1)} %bitcast.9), custom_call_target="tpu_custom_call" | custom-call | tf_op jit(solution)/shard_map/gather_relay/pallas_call | solution.py:217
  11.3 14.0 %attend.1 = (bf16[4096,512]{1,0:T(8,128)(2,1)}, bf16[4096,576]{1,0:T(8,128)(2,1)}, bf16[384,576]{1,0:T(8,128)(2,1)}) custom-call(s32[128]{0:T(128)} %first_ref.1, bf16[4096,576]{1,0:T(8,128)(2,1)} %bitcast.8, bf16[4096,512]{1,0:T(8,128)(2,1)} %bitcast.11, bf16[384,576]{1,0:T(8,128)(2,1)} %get-tuple-element.11.k_ref), custom_call_target="tpu_custom_call" | custom-call | tf_op jit(solution)/shard_map/attend/pallas_call | solution.py:104
  25.3 15.1 %scatter_grads.1 = (f32[64,576]{1,0:T(8,128)}, bf16[32,576,128]{2,1,0:T(8,128)(2,1)}) custom-call(bf16[384,576]{1,0:T(8,128)(2,1)} %get-tuple-element.13.part_ref, bf16[128,32,576]{2,1,0:T(8,128)(2,1)} %bitcast.7), custom_call_target="tpu_custom_call" | custom-call | tf_op jit(solution)/shard_map/scatter_grads/pallas_call | solution.py:331
  40.4 0.0 copy-start
  40.4 4.9 %copy.9 = bf16[128,32,576]{0,2,1:T(8,128)(2,1)} copy(bf16[128,32,576]{0,2,1:T(8,128)(2,1)} %bitcast.10) | data formatting | bytes 9437184
  45.3 0.0 copy-done
  45.3 0.7 %copy.10 = f32[64,576]{1,0:T(8,128)} copy(f32[64,576]{1,0:T(8,128)S(1)} %copy-done) | data formatting | bytes 294912
Async XLA Ops:
  40.4 4.9 %copy-start = (f32[64,576]{1,0:T(8,128)S(1)}, f32[64,576]{1,0:T(8,128)}, u32[]{:S(2)}) copy-start(f32[64,576]{1,0:T(8,128)} %get-tuple-element.22) | copy-start | bytes 442372
where the time goes:
time: 46.4 us; the launch traced here: 46 us
  Pallas kernels  39.8 us (86%)
  local copies, waits for them, and re-layouts  5.55 us (12%)
  between operations  0.66 us (1%)
    pallas_call x1, Pallas kernels, scatter(): pl.pallas_call(partial(scatter_kernel, reach, lax.axis_size('ctx'), head_...  15.1 us
    pallas_call x1, Pallas kernels, attend(): pl.pallas_call(partial(whole_kernel, tokens, heads, span - block_rows), g...  14 us
    pallas_call x1, Pallas kernels, gather(): pl.pallas_call(partial(gather_kernel, reach, lax.axis_size('ctx')), grid=...  10.6 us
    unnamed x4, local copies, waits for them, and re-layouts  5.55 us

commit v1 on v0

--- a/solution.py
+++ b/solution.py
@@ -119,7 +119,7 @@
             jax.ShapeDtypeStruct((span, width), jnp.bfloat16),
         ],
         compiler_params=pltpu.CompilerParams(
-            dimension_semantics=("arbitrary",), vmem_limit_bytes=60 * 1024 * 1024
+            dimension_semantics=("arbitrary",), vmem_limit_bytes=28 * 1024 * 1024
         ),
         name="attend",
     )(doc_start, q, g, keys)
@@ -239,7 +239,7 @@
             dimension_semantics=("arbitrary",),
             collective_id=0,
             has_side_effects=True,
-            vmem_limit_bytes=60 * 1024 * 1024,
+            vmem_limit_bytes=28 * 1024 * 1024,
         ),
         name="gather_relay",
     )(keys, queries)
@@ -353,7 +353,7 @@
             dimension_semantics=("arbitrary",),
             collective_id=1,
             has_side_effects=True,
-            vmem_limit_bytes=60 * 1024 * 1024,
+            vmem_limit_bytes=28 * 1024 * 1024,
         ),
         name="scatter_grads",
     )(partials, d_query)

time: 46.4 us -> 39 us (0.84)
  Pallas kernels: 39.8 us -> 31.7 us
  local copies, waits for them, and re-layouts: 5.55 us -> 6.11 us
    pallas_call x1, Pallas kernels: 15.1 us -> 10.4 us  [scatter(): pl.pallas_call(partial(scatter_kernel, reach, lax.axis_size('ctx'), head_...]
    pallas_call x1, Pallas kernels: 10.6 us -> 8 us  [gather(): pl.pallas_call(partial(gather_kernel, reach, lax.axis_size('ctx')), grid=...]
    pallas_call x1, Pallas kernels: 14 us -> 13.3 us  [attend(): pl.pallas_call(partial(whole_kernel, tokens, heads, span - block_rows), g...]
    unnamed x4 -> x10, local copies, waits for them, and re-layouts: 5.55 us -> 6.11 us
where the time goes in v1:
time: 39 us; the launch traced here: 38.5 us
  Pallas kernels  31.7 us (81%)
  local copies, waits for them, and re-layouts  6.11 us (16%)
  between operations  0.68 us (2%)
    pallas_call x1, Pallas kernels, attend(): pl.pallas_call(partial(whole_kernel, tokens, heads, span - block_rows), g...  13.3 us
    pallas_call x1, Pallas kernels, scatter(): pl.pallas_call(partial(scatter_kernel, reach, lax.axis_size('ctx'), head_...  10.4 us
    pallas_call x1, Pallas kernels, gather(): pl.pallas_call(partial(gather_kernel, reach, lax.axis_size('ctx')), grid=...  8 us
    unnamed x10, local copies, waits for them, and re-layouts  6.11 us

profile of v1, /device:TPU:1, one launch (start us, length us, event | category | flops | bytes accessed | tf_op | source)
XLA Modules:
  0.0 38.5 jit_solution(6172879781847440239)
XLA Ops:
  0.6 0.0 copy-start.3
  0.6 0.0 copy-start
  0.7 2.3 %copy-done = bf16[128,32,576]{0,2,1:T(8,128)(2,1)S(1)} copy-done((bf16[128,32,576]{0,2,1:T(8,128)(2,1)S(1)}, bf16[128,32,576]{0,2,1:T(8,128)(2,1)}, u32[]{:S(2)}) %copy-start) | copy-done | bytes 4718616
  3.0 0.0 copy-start.2
  3.0 0.9 %copy-done.2 = bf16[128,576]{0,1:T(8,128)(2,1)S(1)} copy-done((bf16[128,576]{0,1:T(8,128)(2,1)S(1)}, bf16[128,576]{0,1:T(8,128)(2,1)}, u32[]{:S(2)}) %copy-start.2) | copy-done | bytes 147480
  3.9 0.0 copy-start.1
  3.9 8.0 %gather_relay.1 = (bf16[384,576]{1,0:T(8,128)(2,1)S(1)}, bf16[128,32,576]{2,1,0:T(8,128)(2,1)S(1)}) custom-call(bf16[576,128]{1,0:T(8,128)(2,1)S(1)} %bitcast.12, bf16[32,576,128]{2,1,0:T(8,128)(2,1)S(1)} %bitcast.9), custom_call_target="tpu_custom_call" | custom-call | tf_op jit(solution)/shard_map/gather_relay/pallas_call | solution.py:217
  11.9 0.0 copy-done.3
  11.9 0.0 copy-done.1
  11.9 13.3 %attend.1 = (bf16[4096,512]{1,0:T(8,128)(2,1)}, bf16[4096,576]{1,0:T(8,128)(2,1)S(1)}, bf16[384,576]{1,0:T(8,128)(2,1)S(1)}) custom-call(s32[128]{0:T(128)S(1)} %copy-done.3, bf16[4096,576]{1,0:T(8,128)(2,1)S(1)} %bitcast.8, bf16[4096,512]{1,0:T(8,128)(2,1)S(1)} %bitcast.11, bf16[384,576]{1,0:T(8,128)(2,1)S(1)} %get-tuple-element.11.k_ref), custom_call_target="tpu_custom_call" | custom-call | tf_op jit(solution)/shard_map/attend/pallas_call | solution.py:104
  25.3 10.4 %scatter_grads.1 = (f32[64,576]{1,0:T(8,128)S(1)}, bf16[32,576,128]{2,1,0:T(8,128)(2,1)S(1)}) custom-call(bf16[384,576]{1,0:T(8,128)(2,1)S(1)} %get-tuple-element.13.part_ref, bf16[128,32,576]{2,1,0:T(8,128)(2,1)S(1)} %bitcast.7), custom_call_target="tpu_custom_call" | custom-call | tf_op jit(solution)/shard_map/scatter_grads/pallas_call | solution.py:331
  35.6 2.2 %copy.9 = bf16[128,32,576]{0,2,1:T(8,128)(2,1)} copy(bf16[128,32,576]{0,2,1:T(8,128)(2,1)S(1)} %bitcast.10) | data formatting | bytes 9437184
  37.8 0.7 %copy.10 = f32[64,576]{1,0:T(8,128)} copy(f32[64,576]{1,0:T(8,128)S(1)} %get-tuple-element.22) | data formatting | bytes 294912
Async XLA Ops:
  0.6 11.3 %copy-start.3 = (s32[128]{0:T(128)S(1)}, s32[128]{0:T(128)}, u32[]{:S(2)}) copy-start(s32[128]{0:T(128)} %first_ref.1) | copy-start | bytes 1540
  0.6 2.3 %copy-start = (bf16[128,32,576]{0,2,1:T(8,128)(2,1)S(1)}, bf16[128,32,576]{0,2,1:T(8,128)(2,1)}, u32[]{:S(2)}) copy-start(bf16[128,32,576]{0,2,1:T(8,128)(2,1)} %param.4) | copy-start | bytes 14155780
  3.0 0.9 %copy-start.2 = (bf16[128,576]{0,1:T(8,128)(2,1)S(1)}, bf16[128,576]{0,1:T(8,128)(2,1)}, u32[]{:S(2)}) copy-start(bf16[128,576]{0,1:T(8,128)(2,1)} %param.5) | copy-start | bytes 442372
  3.9 8.0 %copy-start.1 = (bf16[128,32,512]{2,1,0:T(8,128)(2,1)S(1)}, bf16[128,32,512]{2,1,0:T(8,128)(2,1)}, u32[]{:S(2)}) copy-start(bf16[128,32,512]{2,1,0:T(8,128)(2,1)} %param.7) | copy-start | bytes 12582916
